TPU v7x, 256 devices: a whole 4x4x8 slice. The times are simulated.
256 devices in a mesh: energy: 4 (over z_lo), cluster: 16 (over x, y), tile: 4 (over z_hi, core).
Axes of the slice: x: 4, y: 4, z: 8 (z_hi: 2, z_lo: 4; z = z_hi * 4 + z_lo), core: 2. Of those that a mesh axis runs over, the one named last changes fastest.
Arguments:
- boundary: bfloat16 [16, 2, 512, 8, 2, 1024], P('cluster', None, 'tile', 'energy'), may hold values from -5 to 5
- column_source: int32 [16, 1024], P('cluster'), may hold values from 0 to 1023, as said below
- energy_weights: float32 [8], P('energy'), may hold values from 0.2 to 2
Outputs:
- final_rows: float32 [16, 256, 8, 2, 1024], P('cluster', 'tile', 'energy')
- density: float32 [16, 256], P('cluster', 'tile')
Inputs may be any that keep to these rules, and one draw needn't show every extreme that they name: `column_source`: for each cluster, every index 0 to 1023 appears once.
All inputs are finite; a program needn't handle non-finite values.
Results may differ from a plain program's by a relative error of at most 0.015.
Values may be sent and summed in bfloat16 or wider, within the bound.
No kernel may reach another device: no remote copies, remote signals or barrier semaphores. Data moves between devices by JAX's collectives and lax.ppermute only.
A program may use at most 64 MiB of HBM per device.

v0:
```python
import jax
import jax.numpy as jnp
from jax import lax
from jax.sharding import PartitionSpec as P


def swapped(shard, axis, distance):
    return lax.ppermute(shard, axis, [(i, i ^ 1 << distance) for i in range(lax.axis_size(axis))])


def complex_product(left, right):

    def single(first_part, second_part):
        return jnp.einsum(
            "mek,ken->men", first_part, second_part, preferred_element_type=jnp.float32
        )

    real_part = single(left[:, :, 0], right[:, :, 0]) - single(left[:, :, 1], right[:, :, 1])
    imag_part = single(left[:, :, 0], right[:, :, 1]) + single(left[:, :, 1], right[:, :, 0])
    return jnp.stack([real_part, imag_part], axis=2)


def inverse_guess(interior):
    values = interior.astype(jnp.float32)
    diagonal = jnp.diagonal(values, axis1=0, axis2=3)
    denom = diagonal[:, 0] * diagonal[:, 0] + diagonal[:, 1] * diagonal[:, 1]
    inv_real = diagonal[:, 0] / denom
    inv_imag = -diagonal[:, 1] / denom
    column_real = inv_real[None, :, :]
    column_imag = inv_imag[None, :, :]
    row_real = inv_real.T[:, :, None]
    row_imag = inv_imag.T[:, :, None]
    values_real = values[:, :, 0]
    values_imag = values[:, :, 1]
    temp_real = values_real * column_real - values_imag * column_imag
    temp_imag = values_real * column_imag + values_imag * column_real
    prod_real = row_real * temp_real - row_imag * temp_imag
    prod_imag = row_real * temp_imag + row_imag * temp_real
    ident = jnp.eye(values.shape[0], dtype=jnp.float32)[:, None, :]
    guess_real = 2.0 * ident * row_real - prod_real
    guess_imag = 2.0 * ident * row_imag - prod_imag
    return jnp.stack([guess_real, guess_imag], axis=2).astype(jnp.bfloat16)


def place_block(block, is_low):
    zeros = jnp.zeros_like(block)
    return jnp.where(
        is_low, jnp.concatenate([block, zeros], axis=3), jnp.concatenate([zeros, block], axis=3)
    )


def swap_separator(separator, level_index):
    return swapped(separator, "cluster", level_index)


def eliminate(outer_coupling, start_block, interior, approx_inverse, coupling_rows):
    applied = complex_product(outer_coupling.astype(jnp.bfloat16), approx_inverse)
    middle = complex_product(applied.astype(jnp.bfloat16), interior).astype(jnp.bfloat16)
    reduced = (2.0 * applied - complex_product(middle, approx_inverse)).astype(jnp.bfloat16)
    row_piece = lax.all_gather(coupling_rows, "tile", axis=0, tiled=True)
    columns = lax.slice_in_dim(reduced, 0, row_piece.shape[0], axis=3)
    return start_block - complex_product(columns, row_piece)


def per_device(boundary, column_source, energy_weights):
    stored = boundary[0]
    canonical = jnp.take(stored, column_source[0], axis=4)
    separator = canonical[0]
    outer_rows = canonical[1]
    interior_width = separator.shape[3] // 2
    row_count = separator.shape[0]
    levels = min(2, lax.axis_size("cluster") // 2)
    cluster_index = lax.axis_index("cluster")
    tile_index = lax.axis_index("tile")
    for level_index in range(levels):
        side_bit = cluster_index // 2**level_index % 2
        is_low = side_bit == 0
        final_level = level_index == levels - 1
        if final_level:
            partner_outer = outer_rows
            partner_sep = swap_separator(separator, level_index)
        else:
            partner_sep, partner_outer = swapped((separator, outer_rows), "cluster", level_index)
            separator = separator.astype(jnp.float32)
            outer_rows = outer_rows.astype(jnp.float32)
            partner_sep = partner_sep.astype(jnp.float32)
            partner_outer = partner_outer.astype(jnp.float32)
        interior_rows = (
            separator[..., :interior_width] + partner_sep[..., :interior_width]
        ).astype(jnp.bfloat16)
        interior = lax.all_gather(interior_rows, "tile", axis=0, tiled=True)
        approx_inverse = inverse_guess(interior)
        low_sep = jnp.where(is_low, separator, partner_sep)
        high_sep = jnp.where(is_low, partner_sep, separator)
        coupling_rows = jnp.concatenate(
            [low_sep[..., interior_width:], high_sep[..., interior_width:]], axis=3
        ).astype(jnp.bfloat16)
        if final_level:
            share = row_count // 2**level_index
            within = cluster_index % 2**level_index
            own_rows = lax.dynamic_slice_in_dim(outer_rows, within * share, share, 0)
            new_rows = eliminate(
                own_rows[..., :interior_width],
                place_block(own_rows[..., interior_width:], is_low),
                interior,
                approx_inverse,
                coupling_rows,
            )
            columns = (
                side_bit * interior_width
                + tile_index * row_count
                + within * share
                + jnp.arange(share, dtype=jnp.int32)
            )
            selector = (
                jnp.arange(new_rows.shape[3], dtype=jnp.int32)[None, :] == columns[:, None]
            ).astype(jnp.float32)
            diagonal = jnp.sum(new_rows[:, :, 1, :] * selector[:, None, :], axis=2)
            partial_sum = jnp.sum(diagonal * energy_weights[None, :], axis=1)
            density = lax.psum(partial_sum, "energy")
            return (new_rows[None], density[None])
        else:
            low_outer = jnp.where(is_low, outer_rows, partner_outer)
            high_outer = jnp.where(is_low, partner_outer, outer_rows)
            outer_coupling = jnp.concatenate(
                [low_outer[..., :interior_width], high_outer[..., :interior_width]], axis=0
            )
            start_block = jnp.concatenate(
                [
                    place_block(low_outer[..., interior_width:], True),
                    place_block(high_outer[..., interior_width:], False),
                ],
                axis=0,
            )
            merged = eliminate(outer_coupling, start_block, interior, approx_inverse, coupling_rows)
            separator = merged[:row_count]
            outer_rows = merged[row_count:]


def solution(mesh):
    placed = (P("cluster", None, "tile", "energy", None, None), P("cluster", None), P("energy"))
    return jax.shard_map(
        per_device,
        mesh=mesh,
        in_specs=placed,
        out_specs=(P("cluster", "tile", "energy", None, None), P("cluster", "tile")),
        check_vma=False,
    )
```

profile of v0, /device:TPU:2, one launch (start us, length us, event | category | flops | bytes accessed | tf_op | source)
XLA Modules:
  0.0 364.8 jit_solution(14689596253726604121)
XLA Ops:
  7.2 8.9 %copy.65 = bf16[1,2,128,2,2,1024]{2,4,5,3,1,0:T(2,128)(2,1)S(1)} copy(bf16[1,2,128,2,2,1024]{5,4,3,2,1,0:T(2,128)(2,1)} %param.3) | data formatting | bytes 4194304 | tf_op args[0]
  16.2 12.1 %gather_fusion = bf16[1024,2,128,2,2]{2,4,3,1,0:T(2,128)(2,1)} fusion(bf16[2,128,2,2,1024]{1,3,4,2,0:T(2,128)(2,1)S(1)} %bitcast.255, s32[1024]{0:T(1024)S(1)} %broadcast_clamp_fusion), kind=kCustom, calls=%fused_computation | custom fusion | bytes 4198400 | tf_op jit(solution)/shard_map/jit(_take)/gather | solution.py:67
  28.3 6.1 %copy.66 = bf16[1024,2,128,2,2]{0,2,3,4,1:T(8,128)(2,1)} copy(bf16[1024,2,128,2,2]{2,4,3,1,0:T(2,128)(2,1)} %gather_fusion) | data formatting | bytes 4194304 | tf_op jit(solution)/shard_map/jit(_take)/gather | solution.py:67
  34.5 1.8 select_bitcast_fusion
  36.3 1.4 fusion.58
  37.7 1.6 collective-permute-start.1
  39.2 23.3 %collective-permute-done.1 = bf16[128,2,2,1024]{3,0,1,2:T(8,128)(2,1)S(1)} collective-permute-done((bf16[128,2,2,1024]{3,0,1,2:T(8,128)(2,1)S(1)}, bf16[128,2,2,1024]{3,0,1,2:T(8,128)(2,1)S(1)}, u32[]{:S(2)}, u32[]{:S(2)}) %collective-permute-start.1) | collective-permute-done | bytes 1048608 | tf_op jit(solution)/shard_map/ppermute | solution.py:8
  62.8 1.3 copy-done.5
  64.2 1.0 fusion.36
  65.2 1.7 collective-permute-start
  66.9 1.7 select_convert_fusion.3
  68.5 1.1 pad_maximum_fusion.1
  69.9 19.8 %collective-permute-done = bf16[128,2,2,1024]{3,0,1,2:T(8,128)(2,1)} collective-permute-done((bf16[128,2,2,1024]{3,0,1,2:T(8,128)(2,1)}, bf16[128,2,2,1024]{3,0,1,2:T(8,128)(2,1)}, u32[]{:S(2)}, u32[]{:S(2)}) %collective-permute-start) | collective-permute-done | bytes 1048608 | tf_op jit(solution)/shard_map/ppermute | solution.py:8
  89.6 1.8 convert_select_fusion.1
  91.6 1.0 slice.266
  92.7 1.0 slice.267
  93.7 17.7 %all-gather.7.cloned.1.call-done = bf16[512,2,2,512]{3,0,1,2:T(8,128)(2,1)} async-done(((bf16[128,2,2,512]{3,0,1,2:T(8,128)(2,1)}), bf16[512,2,2,512]{3,0,1,2:T(8,128)(2,1)}) %all-gather.7.cloned.1.call-update) | async-done | bytes 2097168 | tf_op jit(solution)/shard_map/all_gather | solution.py:91
  111.5 4.3 %fusion.65 = (f32[512,2,2,512]{3,0,1,2:T(8,128)}, f32[2,2,512,512]{3,2,0,1:T(8,128)S(1)}) fusion(bf16[512,2,2,512]{3,0,1,2:T(8,128)(2,1)} %all-gather.7.cloned.1.call-done), kind=kLoop, calls=%fused_computation.154 | loop fusion | flops 1048576 | bytes 10485760 | tf_op jit(solution)/shard_map/convert_element_type | solution.py:24
  115.7 5.2 %copy.67 = f32[2,2,512,512]{3,1,2,0:T(2,128)} copy(f32[2,2,512,512]{3,2,0,1:T(8,128)S(1)} %get-tuple-element.23) | data formatting | bytes 8388608 | tf_op jit(solution)/shard_map/jit(diagonal)/transpose | solution.py:25
  121.0 7.5 %gather_fusion.1 = f32[512,2,2]{0,2,1:T(2,128)S(1)} fusion(f32[2,2,512,512]{3,1,2,0:T(2,128)} %copy.67, s32[512]{0:T(512)S(1)} %bitcast.253), kind=kCustom, calls=%fused_computation.1 | custom fusion | bytes 20480 | tf_op jit(solution)/shard_map/jit(diagonal)/gather | solution.py:25
  128.5 2.9 fusion.31
  131.4 0.5 fusion.61
  131.9 0.5 fusion.14
  132.4 0.5 fusion.59
  133.0 0.5 fusion.13
  133.7 1.4 copy-done
  135.1 0.5 fusion.38
  135.7 0.5 fusion.18
  136.2 0.5 fusion.68
  136.7 0.5 fusion.39
  137.3 0.5 fusion.17
  137.8 0.5 fusion.12
  138.4 0.5 fusion.69
  138.9 0.5 fusion.11
  139.9 36.3 %all-gather.5.cloned.1.call-done = bf16[512,2,2,1024]{3,0,1,2:T(8,128)(2,1)} async-done(((bf16[128,2,2,1024]{3,0,1,2:T(8,128)(2,1)}), bf16[512,2,2,1024]{3,0,1,2:T(8,128)(2,1)}) %all-gather.5.cloned.1.call-update) | async-done | bytes 4194320 | tf_op jit(solution)/shard_map/all_gather | solution.py:60
  176.1 2.5 fusion.3
  178.9 0.8 fusion.2
  179.7 0.8 subtract_bitcast_fusion
  180.5 0.8 add_bitcast_fusion
  181.3 0.4 copy-done.7
  182.1 0.8 fusion
  182.9 0.6 fusion.63
  183.5 1.3 copy-done.9
  184.8 3.0 collective-permute-start.2
  187.9 46.3 %collective-permute-done.2 = f32[128,2,2,1024]{3,0,1,2:T(8,128)S(1)} collective-permute-done((f32[128,2,2,1024]{3,0,1,2:T(8,128)S(1)}, f32[128,2,2,1024]{3,0,1,2:T(8,128)S(1)}, u32[]{:S(2)}, u32[]{:S(2)}) %collective-permute-start.2) | collective-permute-done | bytes 2097184 | tf_op jit(solution)/shard_map/ppermute | solution.py:8
  234.1 1.3 copy-done.11
  235.4 1.0 fusion.35
  236.5 1.7 select_convert_fusion.1
  238.2 1.1 pad_maximum_fusion.2
  239.4 0.9 dynamic-slice_convert_fusion
  240.3 1.1 constant_dynamic-slice_fusion
  241.4 34.5 %all-gather.11.cloned.1.call-done = bf16[512,2,2,512]{3,0,1,2:T(8,128)(2,1)} async-done(((bf16[128,2,2,512]{3,0,1,2:T(8,128)(2,1)}), bf16[512,2,2,512]{3,0,1,2:T(8,128)(2,1)}) %all-gather.11.cloned.1.call-update) | async-done | bytes 2097168 | tf_op jit(solution)/shard_map/all_gather | solution.py:91
  275.9 4.3 %fusion.64 = (f32[512,2,2,512]{3,0,1,2:T(8,128)}, f32[2,2,512,512]{3,2,0,1:T(8,128)S(1)}) fusion(bf16[512,2,2,512]{3,0,1,2:T(8,128)(2,1)} %all-gather.11.cloned.1.call-done), kind=kLoop, calls=%fused_computation.153 | loop fusion | flops 1048576 | bytes 10485760 | tf_op jit(solution)/shard_map/convert_element_type | solution.py:24
  280.2 5.2 %copy.95 = f32[2,2,512,512]{3,1,2,0:T(2,128)} copy(f32[2,2,512,512]{3,2,0,1:T(8,128)S(1)} %get-tuple-element.21) | data formatting | bytes 8388608 | tf_op jit(solution)/shard_map/jit(diagonal)/transpose | solution.py:25
  285.4 7.2 %gather_fusion.2 = f32[512,2,2]{0,2,1:T(2,128)S(1)} fusion(f32[2,2,512,512]{3,1,2,0:T(2,128)} %copy.95, s32[512]{0:T(512)S(1)} %bitcast.254), kind=kCustom, calls=%fused_computation.2 | custom fusion | bytes 20480 | tf_op jit(solution)/shard_map/jit(diagonal)/gather | solution.py:25
  292.7 2.9 fusion.33
  296.8 0.9 copy-done.1
  300.3 40.8 %all-gather.9.cloned.1.call-done = bf16[512,2,2,1024]{3,0,1,2:T(8,128)(2,1)} async-done(((bf16[128,2,2,1024]{3,0,1,2:T(8,128)(2,1)}), bf16[512,2,2,1024]{3,0,1,2:T(8,128)(2,1)}) %all-gather.9.cloned.1.call-update) | async-done | bytes 4194320 | tf_op jit(solution)/shard_map/all_gather | solution.py:60
  341.0 2.2 fusion.6
  343.3 2.1 fusion.7
  345.4 0.5 fusion.22
  345.8 0.5 fusion.20
  347.2 9.2 %psum.7 = f32[1,64]{1,0:T(1,128)} all-reduce(f32[1,64]{1,0:T(1,128)S(1)} %bitcast.264), channel_id=1, replica_groups=mesh['energy'=4,'cluster'=16,'tile'=4] {'energy'}, use_global_device_ids=true, to_apply=%region_2.3 | all-reduce | flops 64 | bytes 512 | tf_op jit(solution)/shard_map/psum | solution.py:120
  356.5 1.8 copy.99
  (64 shorter events, 6.7 us)
Async XLA Ops:
  7.2 9.0 %copy-start.12 = (s32[1,1024]{1,0:T(1,128)S(1)}, s32[1,1024]{1,0:T(1,128)}, u32[]{:S(2)}) copy-start(s32[1,1024]{1,0:T(1,128)} %param.4) | copy-start | bytes 12292
  7.2 104.3 %all-gather.7.cloned.1.call-start = ((), (), s32[]{:S(2)}) async-start(), calls=%async_computation.1 | async-start | bytes 2621440 | tf_op jit(solution)/shard_map/all_gather | solution.py:91
  37.7 25.2 %copy-start.4 = (f32[128,2,2,1024]{3,0,1,2:T(8,128)}, f32[128,2,2,1024]{3,0,1,2:T(8,128)S(1)}, u32[]{:S(2)}) copy-start(f32[128,2,2,1024]{3,0,1,2:T(8,128)S(1)} %get-tuple-element.24) | copy-start | bytes 6291460
  37.7 24.9 %collective-permute-start.1 = (bf16[128,2,2,1024]{3,0,1,2:T(8,128)(2,1)S(1)}, bf16[128,2,2,1024]{3,0,1,2:T(8,128)(2,1)S(1)}, u32[]{:S(2)}, u32[]{:S(2)}) collective-permute-start(bf16[128,2,2,1024]{3,0,1,2:T(8,128)(2,1)S(1)} %get-tuple-element.25), channel_id=1, source_target_pairs={{0,4},{4,0},{8,12},{12,8},{16,20},{20,16},{24,28},{28,24},{32,36},... | collective-permute-start | bytes 3145736 | tf_op jit(solution)/shard_map/ppermute | solution.py:8
  62.8 1.4 copy-start.5
  65.2 111.0 %all-gather.5.cloned.1.call-start = ((), (), s32[]{:S(2)}) async-start(), calls=%async_computation | async-start | bytes 5242880 | tf_op jit(solution)/shard_map/all_gather | solution.py:60
  65.2 24.4 %collective-permute-start = (bf16[128,2,2,1024]{3,0,1,2:T(8,128)(2,1)}, bf16[128,2,2,1024]{3,0,1,2:T(8,128)(2,1)}, u32[]{:S(2)}, u32[]{:S(2)}) collective-permute-start(bf16[128,2,2,1024]{3,0,1,2:T(8,128)(2,1)} %get-tuple-element.26), channel_id=1, source_target_pairs={{0,4},{4,0},{8,12},{12,8},{16,20},{20,16},{24,28},{28,24},{32,36},... | collective-permute-start | bytes 3145736 | tf_op jit(solution)/shard_map/ppermute | solution.py:8
  69.7 206.3 %all-gather.11.cloned.1.call-start = ((), (), s32[]{:S(2)}) async-start(), calls=%async_computation.3 | async-start | bytes 2621440 | tf_op jit(solution)/shard_map/all_gather | solution.py:91
  133.5 1.6 copy-start
  176.1 2.8 copy-start.3
  180.5 1.2 copy-start.7
  180.5 1.5 copy-start.8
  183.5 1.4 copy-start.9
  183.5 55.9 %copy-start.6 = (f32[128,2,2,1024]{3,0,1,2:T(8,128)}, f32[128,2,2,1024]{3,0,1,2:T(8,128)S(1)}, u32[]{:S(2)}) copy-start(f32[128,2,2,1024]{3,0,1,2:T(8,128)S(1)} %get-tuple-element.12) | copy-start | bytes 6291460
  184.8 49.3 %collective-permute-start.2 = (f32[128,2,2,1024]{3,0,1,2:T(8,128)S(1)}, f32[128,2,2,1024]{3,0,1,2:T(8,128)S(1)}, u32[]{:S(2)}, u32[]{:S(2)}) collective-permute-start(f32[128,2,2,1024]{3,0,1,2:T(8,128)S(1)} %get-tuple-element.13), channel_id=1, source_target_pairs={{0,8},{4,12},{8,0},{12,4},{16,24},{20,28},{24,16},{28,20},{32,40},... | collective-permute-start | bytes 6291464 | tf_op jit(solution)/shard_map/ppermute | solution.py:8
  234.1 1.3 copy-start.11
  236.4 104.6 %all-gather.9.cloned.1.call-start = ((), (), s32[]{:S(2)}) async-start(), calls=%async_computation.2 | async-start | bytes 5242880 | tf_op jit(solution)/shard_map/all_gather | solution.py:60
  292.6 2.9 copy-start.10
  296.2 1.6 copy-start.1
  341.0 4.3 %copy-start.2 = (bf16[512,2,2,1024]{3,0,1,2:T(8,128)(2,1)S(1)}, bf16[512,2,2,1024]{3,0,1,2:T(8,128)(2,1)}, u32[]{:S(2)}) copy-start(bf16[512,2,2,1024]{3,0,1,2:T(8,128)(2,1)} %all-gather.9.cloned.1.call-done) | copy-start | bytes 12582916
  346.5 0.7 copy-start.13
Sparse Core Ops, SparseCore 0:
  65.3 46.1 all-gather.6
  113.3 62.8 all-gather.4
  236.6 39.3 all-gather.10
  278.2 62.8 all-gather.8
where the time goes:
time: 366 us; the launch traced here: 365 us
  waiting for transfers between devices  219 us (60%)
  local copies, waits for them, and re-layouts  66.7 us (18%)
  other arithmetic  29.4 us (8%)
  matrix products  20.1 us (5%)
  between operations  14.3 us (4%)
  blocking collectives  9.25 us (3%)
  starting transfers between devices  6.4 us (2%)
    ppermute x3, waiting for transfers between devices, swapped(): lax.ppermute(shard, axis, [(i, i ^ 1 << distance) for i in range(lax.axis...  89.4 us
    all_gather x2, waiting for transfers between devices, eliminate(): row_piece = lax.all_gather(coupling_rows, 'tile', axis=0, tiled=True)  77 us
    all_gather x2, waiting for transfers between devices, per_device(): interior = lax.all_gather(interior_rows, 'tile', axis=0, tiled=True)  52.2 us
    dot_general x32, matrix products, single(): jnp.einsum('mek,ken->men', first_part, second_part, preferred_element_typ...  20.1 us
    unnamed x30, local copies, waits for them, and re-layouts  18.5 us
    gather x2, local copies, waits for them, and re-layouts, per_device(): canonical = jnp.take(stored, column_source[0], axis=4)  18.3 us
    gather x2, local copies, waits for them, and re-layouts, inverse_guess(): diagonal = jnp.diagonal(values, axis1=0, axis2=3)  14.7 us
    transpose x2, local copies, waits for them, and re-layouts, inverse_guess(): diagonal = jnp.diagonal(values, axis1=0, axis2=3)  10.5 us
  transfers between devices with their start and end apart: 7, of which 7 were waited for; matrix products, arithmetic and copies ran while one was open for 17% of the time, Pallas kernels for 0%

commit v1 on v0

--- a/solution.py
+++ b/solution.py
@@ -2,6 +2,13 @@
 import jax.numpy as jnp
 from jax import lax
 from jax.sharding import PartitionSpec as P
+
+
+def part_arrays(payload):
+    frames = []
+    for _ in range(lax.axis_size("tile")):
+        frames.append(payload)
+    return jnp.concatenate(lax.all_to_all(jnp.stack(frames, 0), "tile", 0, 0), 0)
 
 
 def swapped(shard, axis, distance):
@@ -57,7 +64,7 @@
     applied = complex_product(outer_coupling.astype(jnp.bfloat16), approx_inverse)
     middle = complex_product(applied.astype(jnp.bfloat16), interior).astype(jnp.bfloat16)
     reduced = (2.0 * applied - complex_product(middle, approx_inverse)).astype(jnp.bfloat16)
-    row_piece = lax.all_gather(coupling_rows, "tile", axis=0, tiled=True)
+    row_piece = part_arrays(coupling_rows)
     columns = lax.slice_in_dim(reduced, 0, row_piece.shape[0], axis=3)
     return start_block - complex_product(columns, row_piece)
 

time: 366 us -> 414 us (1.13)
  waiting for transfers between devices: 219 us -> 245 us
  starting transfers between devices: 6.4 us -> 16.6 us
  blocking collectives: 9.25 us -> 18.7 us
  local copies, waits for them, and re-layouts: 66.7 us -> 75.6 us
  matrix products: 20.1 us -> 15.1 us
    all_to_all x0 -> x2, waiting for transfers between devices: none -> 99.6 us  [part_arrays(): lax.all_to_all(jnp.stack(frames, 0), 'tile', 0, 0)]
    all_gather x2 -> x0, waiting for transfers between devices: 77 us -> none  [eliminate(): row_piece = lax.all_gather(coupling_rows, 'tile', axis=0, tiled=True)]
    all_to_all x0 -> x2, starting transfers between devices: none -> 13.3 us  [part_arrays(): lax.all_to_all(jnp.stack(frames, 0), 'tile', 0, 0)]
    all_gather x2, waiting for transfers between devices: 52.2 us -> 63.4 us  [per_device(): interior = lax.all_gather(interior_rows, 'tile', axis=0, tiled=True)]
    psum x1, blocking collectives: 9.25 us -> 18.7 us  [per_device(): density = lax.psum(partial_sum, 'energy')]
    ppermute x3, waiting for transfers between devices: 89.4 us -> 81.6 us  [swapped(): lax.ppermute(shard, axis, [(i, i ^ 1 << distance) for i in range(lax.axis...]
    all_to_all x0 -> x2, local copies, waits for them, and re-layouts: none -> 5.26 us  [part_arrays(): lax.all_to_all(jnp.stack(frames, 0), 'tile', 0, 0)]
    another operation x1 -> x3, local copies, waits for them, and re-layouts: 0.9 us -> 6.13 us  [the longest x2 5.23 us: part_arrays(): jnp.stack(frames, 0)]
  transfers between devices with their start and end apart: 7 -> 7, of which waited for: 7 -> 7; matrix products, arithmetic and copies ran while one was open for 17% -> 16% of each run, Pallas kernels for 0% -> 0%
where the time goes in v1:
time: 414 us; the launch traced here: 412 us
  waiting for transfers between devices  245 us (59%)
  local copies, waits for them, and re-layouts  75.6 us (18%)
  other arithmetic  27.3 us (7%)
  blocking collectives  18.7 us (5%)
  starting transfers between devices  16.6 us (4%)
  matrix products  15.1 us (4%)
  between operations  14.6 us (4%)
    all_to_all x2, waiting for transfers between devices, part_arrays(): lax.all_to_all(jnp.stack(frames, 0), 'tile', 0, 0)  99.6 us
    ppermute x3, waiting for transfers between devices, swapped(): lax.ppermute(shard, axis, [(i, i ^ 1 << distance) for i in range(lax.axis...  81.6 us
    all_gather x2, waiting for transfers between devices, per_device(): interior = lax.all_gather(interior_rows, 'tile', axis=0, tiled=True)  63.4 us
    psum x1, blocking collectives, per_device(): density = lax.psum(partial_sum, 'energy')  18.7 us
    gather x2, local copies, waits for them, and re-layouts, per_device(): canonical = jnp.take(stored, column_source[0], axis=4)  18.3 us
    unnamed x26, local copies, waits for them, and re-layouts  18.1 us
    dot_general x32, matrix products, single(): jnp.einsum('mek,ken->men', first_part, second_part, preferred_element_typ...  15.1 us
    gather x2, local copies, waits for them, and re-layouts, inverse_guess(): diagonal = jnp.diagonal(values, axis1=0, axis2=3)  13.6 us
  transfers between devices with their start and end apart: 7, of which 7 were waited for; matrix products, arithmetic and copies ran while one was open for 16% of the time, Pallas kernels for 0%

profile of v1, /device:TPU:2, one launch (start us, length us, event | category | flops | bytes accessed | tf_op | source)
XLA Modules:
  0.0 412.5 jit_solution(1801200762063886548)
XLA Ops:
  7.2 8.9 %copy.65 = bf16[1,2,128,2,2,1024]{2,4,5,3,1,0:T(2,128)(2,1)S(1)} copy(bf16[1,2,128,2,2,1024]{5,4,3,2,1,0:T(2,128)(2,1)} %param.3) | data formatting | bytes 4194304 | tf_op args[0]
  16.2 12.1 %gather_fusion = bf16[1024,2,128,2,2]{2,4,3,1,0:T(2,128)(2,1)} fusion(bf16[2,128,2,2,1024]{1,3,4,2,0:T(2,128)(2,1)S(1)} %bitcast.265, s32[1024]{0:T(1024)S(1)} %broadcast_clamp_fusion), kind=kCustom, calls=%fused_computation | custom fusion | bytes 4198400 | tf_op jit(solution)/shard_map/jit(_take)/gather | solution.py:74
  28.3 6.2 %copy.66 = bf16[1024,2,128,2,2]{0,2,3,4,1:T(8,128)(2,1)} copy(bf16[1024,2,128,2,2]{2,4,3,1,0:T(2,128)(2,1)} %gather_fusion) | data formatting | bytes 4194304 | tf_op jit(solution)/shard_map/jit(_take)/gather | solution.py:74
  34.5 1.8 select_bitcast_fusion
  36.3 1.4 fusion.58
  37.7 1.6 collective-permute-start.1
  39.3 23.3 %collective-permute-done.1 = bf16[128,2,2,1024]{3,0,1,2:T(8,128)(2,1)S(1)} collective-permute-done((bf16[128,2,2,1024]{3,0,1,2:T(8,128)(2,1)S(1)}, bf16[128,2,2,1024]{3,0,1,2:T(8,128)(2,1)S(1)}, u32[]{:S(2)}, u32[]{:S(2)}) %collective-permute-start.1) | collective-permute-done | bytes 1048608 | tf_op jit(solution)/shard_map/ppermute | solution.py:15
  62.8 1.3 copy-done.3
  64.2 0.9 fusion.36
  65.1 1.7 collective-permute-start
  66.8 1.7 select_convert_fusion.3
  68.6 2.6 stack.88
  71.2 8.5 %all-to-all-start = ((bf16[4,128,2,2,1024]{4,1,2,3,0:T(8,128)(2,1)}), bf16[4,128,2,2,1024]{4,1,2,3,0:T(8,128)(2,1)}, u32[]{:S(2)}, u32[]{:S(2)}) async-start(bf16[4,128,2,2,1024]{4,1,2,3,0:T(8,128)(2,1)} %stack.88), calls=%async_computation | async-start | bytes 8388608 | tf_op jit(solution)/shard_map/all_to_all | solution.py:11
  79.8 9.8 %collective-permute-done = bf16[128,2,2,1024]{3,0,1,2:T(8,128)(2,1)} collective-permute-done((bf16[128,2,2,1024]{3,0,1,2:T(8,128)(2,1)}, bf16[128,2,2,1024]{3,0,1,2:T(8,128)(2,1)}, u32[]{:S(2)}, u32[]{:S(2)}) %collective-permute-start) | collective-permute-done | bytes 1048608 | tf_op jit(solution)/shard_map/ppermute | solution.py:15
  89.6 1.8 convert_select_fusion.1
  91.5 1.1 slice.266
  92.6 1.0 slice.267
  93.7 24.8 %all-gather.3.cloned.1.call-done = bf16[512,2,2,512]{3,0,1,2:T(8,128)(2,1)} async-done(((bf16[128,2,2,512]{3,0,1,2:T(8,128)(2,1)}), bf16[512,2,2,512]{3,0,1,2:T(8,128)(2,1)}) %all-gather.3.cloned.1.call-update) | async-done | bytes 2097168 | tf_op jit(solution)/shard_map/all_gather | solution.py:98
  118.5 4.2 %fusion.65 = (f32[512,2,2,512]{3,0,1,2:T(8,128)}, f32[2,2,512,512]{3,2,0,1:T(8,128)S(1)}) fusion(bf16[512,2,2,512]{3,0,1,2:T(8,128)(2,1)} %all-gather.3.cloned.1.call-done), kind=kLoop, calls=%fused_computation.154 | loop fusion | flops 1048576 | bytes 10485760 | tf_op jit(solution)/shard_map/convert_element_type | solution.py:31
  122.7 5.2 %copy.68 = f32[2,2,512,512]{3,1,2,0:T(2,128)} copy(f32[2,2,512,512]{3,2,0,1:T(8,128)S(1)} %get-tuple-element.23) | data formatting | bytes 8388608 | tf_op jit(solution)/shard_map/jit(diagonal)/transpose | solution.py:32
  127.9 6.8 %gather_fusion.1 = f32[512,2,2]{0,2,1:T(2,128)S(1)} fusion(f32[2,2,512,512]{3,1,2,0:T(2,128)} %copy.68, s32[512]{0:T(512)S(1)} %bitcast.255), kind=kCustom, calls=%fused_computation.1 | custom fusion | bytes 20480 | tf_op jit(solution)/shard_map/jit(diagonal)/gather | solution.py:32
  134.7 2.9 fusion.31
  137.6 0.5 fusion.61
  138.1 0.5 fusion.14
  138.7 0.5 fusion.59
  139.2 0.5 fusion.13
  140.0 1.4 copy-done
  141.4 0.5 fusion.38
  141.9 0.5 fusion.18
  142.4 0.5 fusion.68
  143.0 0.5 fusion.39
  143.5 0.5 fusion.17
  144.1 0.5 fusion.12
  144.6 0.5 fusion.69
  145.1 0.5 fusion.11
  146.1 52.9 %all-to-all-done = bf16[4,128,2,2,1024]{4,1,2,3,0:T(8,128)(2,1)} async-done(((bf16[4,128,2,2,1024]{4,1,2,3,0:T(8,128)(2,1)}), bf16[4,128,2,2,1024]{4,1,2,3,0:T(8,128)(2,1)}, u32[]{:S(2)}, u32[]{:S(2)}) %all-to-all-start) | async-done | bytes 4194336 | tf_op jit(solution)/shard_map/all_to_all | solution.py:11
  199.0 2.6 copy.67
  201.6 0.8 fusion.3
  202.4 0.8 fusion.2
  203.2 0.8 subtract_bitcast_fusion
  204.0 0.8 add_bitcast_fusion
  205.5 0.7 fusion
  206.3 0.6 fusion.63
  206.9 1.3 copy-done.7
  208.2 48.5 %collective-permute-done.2 = f32[128,2,2,1024]{3,0,1,2:T(8,128)S(1)} collective-permute-done((f32[128,2,2,1024]{3,0,1,2:T(8,128)S(1)}, f32[128,2,2,1024]{3,0,1,2:T(8,128)S(1)}, u32[]{:S(2)}, u32[]{:S(2)}) %collective-permute-start.2) | collective-permute-done | bytes 2097184 | tf_op jit(solution)/shard_map/ppermute | solution.py:15
  256.7 1.3 copy-done.9
  258.0 1.0 fusion.35
  259.0 1.7 select_convert_fusion.1
  260.8 2.6 stack.98
  263.5 4.9 %all-to-all-start.1 = ((bf16[4,128,2,2,1024]{4,1,2,3,0:T(8,128)(2,1)}), bf16[4,128,2,2,1024]{4,1,2,3,0:T(8,128)(2,1)}, u32[]{:S(2)}, u32[]{:S(2)}) async-start(bf16[4,128,2,2,1024]{4,1,2,3,0:T(8,128)(2,1)} %stack.98), calls=%async_computation.1 | async-start | bytes 8388608 | tf_op jit(solution)/shard_map/all_to_all | solution.py:11
  268.4 0.9 dynamic-slice_convert_fusion
  269.3 1.1 constant_dynamic-slice_fusion
  270.4 38.6 %all-gather.5.cloned.1.call-done = bf16[512,2,2,512]{3,0,1,2:T(8,128)(2,1)} async-done(((bf16[128,2,2,512]{3,0,1,2:T(8,128)(2,1)}), bf16[512,2,2,512]{3,0,1,2:T(8,128)(2,1)}) %all-gather.5.cloned.1.call-update) | async-done | bytes 2097168 | tf_op jit(solution)/shard_map/all_gather | solution.py:98
  309.0 4.2 %fusion.64 = (f32[512,2,2,512]{3,0,1,2:T(8,128)}, f32[2,2,512,512]{3,2,0,1:T(8,128)S(1)}) fusion(bf16[512,2,2,512]{3,0,1,2:T(8,128)(2,1)} %all-gather.5.cloned.1.call-done), kind=kLoop, calls=%fused_computation.153 | loop fusion | flops 1048576 | bytes 10485760 | tf_op jit(solution)/shard_map/convert_element_type | solution.py:31
  313.2 5.2 %copy.97 = f32[2,2,512,512]{3,1,2,0:T(2,128)} copy(f32[2,2,512,512]{3,2,0,1:T(8,128)S(1)} %get-tuple-element.21) | data formatting | bytes 8388608 | tf_op jit(solution)/shard_map/jit(diagonal)/transpose | solution.py:32
  318.4 6.8 %gather_fusion.2 = f32[512,2,2]{0,2,1:T(2,128)S(1)} fusion(f32[2,2,512,512]{3,1,2,0:T(2,128)} %copy.97, s32[512]{0:T(512)S(1)} %bitcast.256), kind=kCustom, calls=%fused_computation.2 | custom fusion | bytes 20480 | tf_op jit(solution)/shard_map/jit(diagonal)/gather | solution.py:32
  325.3 2.9 fusion.33
  329.4 0.9 copy-done.1
  332.9 46.7 %all-to-all-done.1 = bf16[4,128,2,2,1024]{4,1,2,3,0:T(8,128)(2,1)} async-done(((bf16[4,128,2,2,1024]{4,1,2,3,0:T(8,128)(2,1)}), bf16[4,128,2,2,1024]{4,1,2,3,0:T(8,128)(2,1)}, u32[]{:S(2)}, u32[]{:S(2)}) %all-to-all-start.1) | async-done | bytes 4194336 | tf_op jit(solution)/shard_map/all_to_all | solution.py:11
  379.6 2.6 copy.96
  383.2 0.5 fusion.22
  383.7 0.5 fusion.20
  385.1 18.7 %psum.7 = f32[1,64]{1,0:T(1,128)} all-reduce(f32[1,64]{1,0:T(1,128)S(1)} %bitcast.274), channel_id=1, replica_groups=mesh['energy'=4,'cluster'=16,'tile'=4] {'energy'}, use_global_device_ids=true, to_apply=%region_2.3 | all-reduce | flops 64 | bytes 512 | tf_op jit(solution)/shard_map/psum | solution.py:127
  403.9 1.8 copy.101
  (62 shorter events, 7.9 us)
Async XLA Ops:
  7.2 9.0 %copy-start.10 = (s32[1,1024]{1,0:T(1,128)S(1)}, s32[1,1024]{1,0:T(1,128)}, u32[]{:S(2)}) copy-start(s32[1,1024]{1,0:T(1,128)} %param.4) | copy-start | bytes 12292
  7.2 111.3 %all-gather.3.cloned.1.call-start = ((), (), s32[]{:S(2)}) async-start(), calls=%async_computation.2 | async-start | bytes 2621440 | tf_op jit(solution)/shard_map/all_gather | solution.py:98
  37.7 25.2 %copy-start.2 = (f32[128,2,2,1024]{3,0,1,2:T(8,128)}, f32[128,2,2,1024]{3,0,1,2:T(8,128)S(1)}, u32[]{:S(2)}) copy-start(f32[128,2,2,1024]{3,0,1,2:T(8,128)S(1)} %get-tuple-element.24) | copy-start | bytes 6291460
  37.7 24.9 %collective-permute-start.1 = (bf16[128,2,2,1024]{3,0,1,2:T(8,128)(2,1)S(1)}, bf16[128,2,2,1024]{3,0,1,2:T(8,128)(2,1)S(1)}, u32[]{:S(2)}, u32[]{:S(2)}) collective-permute-start(bf16[128,2,2,1024]{3,0,1,2:T(8,128)(2,1)S(1)} %get-tuple-element.25), channel_id=1, source_target_pairs={{0,4},{4,0},{8,12},{12,8},{16,20},{20,16},{24,28},{28,24},{32,36},... | collective-permute-start | bytes 3145736 | tf_op jit(solution)/shard_map/ppermute | solution.py:15
  62.8 1.3 copy-start.3
  65.1 24.4 %collective-permute-start = (bf16[128,2,2,1024]{3,0,1,2:T(8,128)(2,1)}, bf16[128,2,2,1024]{3,0,1,2:T(8,128)(2,1)}, u32[]{:S(2)}, u32[]{:S(2)}) collective-permute-start(bf16[128,2,2,1024]{3,0,1,2:T(8,128)(2,1)} %get-tuple-element.26), channel_id=1, source_target_pairs={{0,4},{4,0},{8,12},{12,8},{16,20},{20,16},{24,28},{28,24},{32,36},... | collective-permute-start | bytes 3145736 | tf_op jit(solution)/shard_map/ppermute | solution.py:15
  71.2 127.8 %all-to-all-start = ((bf16[4,128,2,2,1024]{4,1,2,3,0:T(8,128)(2,1)}), bf16[4,128,2,2,1024]{4,1,2,3,0:T(8,128)(2,1)}, u32[]{:S(2)}, u32[]{:S(2)}) async-start(bf16[4,128,2,2,1024]{4,1,2,3,0:T(8,128)(2,1)} %stack.88), calls=%async_computation | async-start | bytes 8388608 | tf_op jit(solution)/shard_map/all_to_all | solution.py:11
  79.7 229.3 %all-gather.5.cloned.1.call-start = ((), (), s32[]{:S(2)}) async-start(), calls=%async_computation.3 | async-start | bytes 2621440 | tf_op jit(solution)/shard_map/all_gather | solution.py:98
  139.8 1.6 copy-start
  204.0 1.2 copy-start.5
  204.0 1.5 copy-start.6
  206.8 1.3 copy-start.7
  206.9 61.6 %copy-start.4 = (f32[128,2,2,1024]{3,0,1,2:T(8,128)}, f32[128,2,2,1024]{3,0,1,2:T(8,128)S(1)}, u32[]{:S(2)}) copy-start(f32[128,2,2,1024]{3,0,1,2:T(8,128)S(1)} %get-tuple-element.12) | copy-start | bytes 6291460
  208.2 48.5 %collective-permute-start.2 = (f32[128,2,2,1024]{3,0,1,2:T(8,128)S(1)}, f32[128,2,2,1024]{3,0,1,2:T(8,128)S(1)}, u32[]{:S(2)}, u32[]{:S(2)}) collective-permute-start(f32[128,2,2,1024]{3,0,1,2:T(8,128)S(1)} %get-tuple-element.13), channel_id=1, source_target_pairs={{0,8},{4,12},{8,0},{12,4},{16,24},{20,28},{24,16},{28,20},{32,40},... | collective-permute-start | bytes 6291464 | tf_op jit(solution)/shard_map/ppermute | solution.py:15
  256.7 1.3 copy-start.9
  263.5 116.1 %all-to-all-start.1 = ((bf16[4,128,2,2,1024]{4,1,2,3,0:T(8,128)(2,1)}), bf16[4,128,2,2,1024]{4,1,2,3,0:T(8,128)(2,1)}, u32[]{:S(2)}, u32[]{:S(2)}) async-start(bf16[4,128,2,2,1024]{4,1,2,3,0:T(8,128)(2,1)} %stack.98), calls=%async_computation.1 | async-start | bytes 8388608 | tf_op jit(solution)/shard_map/all_to_all | solution.py:11
  325.3 2.9 copy-start.8
  328.8 1.6 copy-start.1
  384.4 0.7 copy-start.11
Sparse Core Ops, SparseCore 0:
  65.3 53.1 all-gather.2
  259.1 49.8 all-gather.4
